TPU v7x, 256 devices: a whole 4x4x8 slice. The times are simulated.
256 devices in a mesh: grp: 4 (over y_hi, core), fsdp: 64 (over y_lo, x, z).
Axes of the slice: x: 4, y: 4 (y_hi: 2, y_lo: 2; y = y_hi * 2 + y_lo), z: 8, core: 2. Of those that a mesh axis runs over, the one named last changes fastest.
Arguments:
- traj_hidden: bfloat16 [262144, 4096], P(('grp', 'fsdp')), may hold values from -24 to 24
- traj_tokens: int32 [262144], P(('grp', 'fsdp')), may hold values from 0 to 511
- traj_action: int32 [262144], P(('grp', 'fsdp')), may hold values from 0 to 511
- traj_return: float32 [262144], P(('grp', 'fsdp')), may hold values from -6 to 6
- traj_episode: int32 [256, 1024], P(('grp', 'fsdp')), may hold values from 0 to 7, never falling along the last dimension, each value on 1 to 512 neighbouring positions
- roll_hidden: bfloat16 [16384, 4096], P(('grp', 'fsdp')), may hold values from -6 to 6
- roll_tokens: int32 [16384], P(('grp', 'fsdp')), may hold values from 0 to 511
- roll_action: int32 [16384], P(('grp', 'fsdp')), may hold values from 0 to 511
- station_table: bfloat16 [512, 4096], replicated, may hold values from -3 to 3
- norm_gain: float32 [4096], replicated, may hold values from 0.7 to 3.9
- head_weight: bfloat16 [4096, 512], P('fsdp'), may hold values from -6 to 6
Outputs:
- new_head: bfloat16 [4096, 512], P('fsdp')
- action_logp: float32 [16384], P(('grp', 'fsdp'))
- episode_logp: float32 [256], P(('grp', 'fsdp'))
Inputs may be any that keep to these rules, and one draw needn't show every extreme that they name: `traj_episode`: within each block of 1024 tokens the episode numbers never fall and every number 0 to 7 occurs.
All inputs are finite; a program needn't handle non-finite values.
Results may differ from a plain program's by a relative error of at most 0.0034.
Values may be sent and summed in bfloat16 or wider, within the bound.
A program may use at most 64 MiB of HBM per device.

v0:
```python
import jax
import jax.numpy as jnp
from jax import lax
from jax.sharding import PartitionSpec as P

ACTIONS = 512
STATIONS = 512
EPI_BLK = 8
STEPS = 64


step_length = 8.0


def station_rows(hidden, tokens, table, gain):
    lookup = (tokens[:, None] == jnp.arange(STATIONS, dtype=jnp.int32)[None, :]).astype(
        jnp.bfloat16
    )
    embedded = jnp.dot(lookup, table, preferred_element_type=jnp.float32)
    mixed = hidden.astype(jnp.float32) + embedded
    power = jnp.mean(mixed * mixed, axis=-1, keepdims=True)
    return (mixed * lax.rsqrt(power + 1e-05) * gain).astype(jnp.bfloat16)


def add_columns(left, piece):
    return jnp.dot(left, piece, preferred_element_type=jnp.float32)


def picked_logp(logits, actions):
    top = jnp.max(logits, axis=-1, keepdims=True)
    total = jnp.log(jnp.sum(jnp.exp(logits - top), axis=-1)) + top[:, 0]
    chosen = (actions[:, None] == jnp.arange(ACTIONS, dtype=jnp.int32)[None, :]).astype(jnp.float32)
    return jnp.sum(logits * chosen, axis=-1) - total


def episode_advantage(returns, episode):
    member = (episode[:, None] == jnp.arange(EPI_BLK, dtype=jnp.int32)[None, :]).astype(jnp.float32)
    sums = jnp.dot(member.T, returns, precision=lax.Precision.HIGHEST)
    counts = jnp.sum(member, axis=0)
    baseline = jnp.dot(member, sums / counts, precision=lax.Precision.HIGHEST)
    return returns - baseline


def outer_rows(left, right):
    return lax.dot_general(
        left, right, (((0,), (0,)), ((), ())), preferred_element_type=jnp.float32
    )


def local(
    traj_hidden,
    traj_tokens,
    traj_action,
    traj_return,
    traj_episode,
    roll_hidden,
    roll_tokens,
    roll_action,
    station_table,
    norm_gain,
    head_weight,
):
    features = station_rows(traj_hidden, traj_tokens, station_table, norm_gain)
    rollout = station_rows(roll_hidden, roll_tokens, station_table, norm_gain)
    advantage = episode_advantage(traj_return, traj_episode[0])
    logits = add_columns(features, lax.all_gather(head_weight, "fsdp", axis=0, tiled=True))
    top = jnp.max(logits, axis=-1, keepdims=True)
    expo = jnp.exp(logits - top)
    probs = expo / jnp.sum(expo, axis=-1, keepdims=True)
    chosen = (traj_action[:, None] == jnp.arange(ACTIONS, dtype=jnp.int32)[None, :]).astype(
        jnp.float32
    )
    scores = (advantage[:, None] * (probs - chosen)).astype(jnp.bfloat16)
    gathered, all_scores = (features, scores)
    grad_shard = lax.psum_scatter(
        outer_rows(gathered, all_scores), "fsdp", scatter_dimension=0, tiled=True
    )
    grad_shard = lax.psum(grad_shard, "grp")
    squares = lax.psum(jnp.sum(grad_shard * grad_shard), "fsdp")
    gnorm = jnp.sqrt(squares + 1e-06)
    new_head = (head_weight.astype(jnp.float32) - step_length * grad_shard / gnorm).astype(
        jnp.bfloat16
    )
    roll_logits = add_columns(rollout, lax.all_gather(new_head, "fsdp", axis=0, tiled=True))
    action_logp = picked_logp(roll_logits, roll_action)
    episode_logp = jnp.sum(action_logp.reshape(-1, STEPS), axis=1)
    return (new_head, action_logp, episode_logp)


def solution(mesh):
    placed = (
        P(("grp", "fsdp"), None),
        P(("grp", "fsdp")),
        P(("grp", "fsdp")),
        P(("grp", "fsdp")),
        P(("grp", "fsdp"), None),
        P(("grp", "fsdp"), None),
        P(("grp", "fsdp")),
        P(("grp", "fsdp")),
        P(),
        P(),
        P("fsdp", None),
    )
    return jax.shard_map(
        local,
        mesh=mesh,
        in_specs=placed,
        out_specs=(P("fsdp", None), P(("grp", "fsdp")), P(("grp", "fsdp"))),
        check_vma=False,
    )
```

profile of v0, /device:TPU:16, one launch (start us, length us, event | category | flops | bytes accessed | tf_op | source)
XLA Modules:
  0.0 1174.0 jit_solution(12649572377093902791)
XLA Ops:
  7.2 0.7 all-gather.3.cloned.1.call-update
  7.9 0.0 reduce-scatter.2.cloned.1.call-start
  7.9 0.8 convert_reduce_fusion
  8.8 0.8 fusion.3
  9.6 0.9 fusion.14
  10.4 0.7 sub.30
  11.1 8.8 multiply_reduce_fusion
  20.0 8.9 multiply_convert_fusion
  28.8 287.5 %all-gather.3.cloned.1.call-done = bf16[4096,512]{1,0:T(8,128)(2,1)} async-done(((bf16[64,512]{1,0:T(8,128)(2,1)}), bf16[4096,512]{1,0:T(8,128)(2,1)}) %all-gather.3.cloned.1.call-update) | async-done | bytes 4194320 | tf_op jit(solution)/shard_map/all_gather | solution.py:66
  316.3 8.4 fusion.18
  324.7 0.3 fusion.1
  325.1 7.7 fusion.4
  332.8 0.0 all-reduce.2.cloned.1.call-start
  332.8 329.6 %reduce-scatter.2.cloned.1.call-done = f32[64,512]{1,0:T(8,128)} async-done(((f32[4096,512]{1,0:T(8,128)}), f32[64,512]{1,0:T(8,128)}) %reduce-scatter.2.cloned.1.call-update) | async-done | bytes 131088 | tf_op jit(solution)/shard_map/reduce_scatter | solution.py:75
  662.5 0.0 all-gather.5.cloned.1.call-start
  662.5 39.2 %all-reduce.2.cloned.1.call-done = f32[64,512]{1,0:T(8,128)} async-done(((f32[64,512]{1,0:T(8,128)}), f32[64,512]{1,0:T(8,128)}) %all-reduce.2.cloned.1.call-update) | async-done | bytes 131088 | tf_op jit(solution)/shard_map/psum | solution.py:78
  701.7 1.5 multiply_reduce_fusion.2
  703.3 159.9 %psum.15 = f32[]{:T(128)} all-reduce(f32[]{:T(128)} %multiply_reduce_fusion.2), channel_id=1, replica_groups=mesh['grp'=4,'fsdp'=64] {'fsdp'}, use_global_device_ids=true, to_apply=%region_7.0 | all-reduce | flops 1 | bytes 8 | tf_op jit(solution)/shard_map/psum | solution.py:79
  863.8 1.6 subtract_convert_fusion
  865.4 3.2 multiply_reduce_fusion.1
  868.7 294.3 %all-gather.5.cloned.1.call-done = bf16[4096,512]{1,0:T(8,128)(2,1)} async-done(((bf16[64,512]{1,0:T(8,128)(2,1)}), bf16[4096,512]{1,0:T(8,128)(2,1)}) %all-gather.5.cloned.1.call-update) | async-done | bytes 4194320 | tf_op jit(solution)/shard_map/all_gather | solution.py:84
  1163.0 3.2 fusion.19
  1166.2 0.2 exponential_reduce_fusion
  1166.4 1.1 fusion.17
  (20 shorter events, 0.1 us)
Async XLA Ops:
  7.2 309.2 %all-gather.3.cloned.1.call-start = ((), (), s32[]{:S(2)}) async-start(), calls=%async_computation.1 | async-start | bytes 4259840 | tf_op jit(solution)/shard_map/all_gather | solution.py:66
  7.9 654.5 %reduce-scatter.2.cloned.1.call-start = ((), (), s32[]{:S(2)}) async-start(), calls=%async_computation.2 | async-start | bytes 8519680 | tf_op jit(solution)/shard_map/reduce_scatter | solution.py:75
  11.1 8.8 copy-start.3
  28.8 296.3 %copy-start.6 = (s32[1024]{0:T(1024)S(1)}, s32[1024]{0:T(1024)}, u32[]{:S(2)}) copy-start(s32[1024]{0:T(1024)} %param.13) | copy-start | bytes 12292
  316.3 8.8 copy-start
  332.7 531.1 %copy-start.2 = (bf16[64,512]{1,0:T(8,128)(2,1)S(1)}, bf16[64,512]{1,0:T(8,128)(2,1)}, u32[]{:S(2)}) copy-start(bf16[64,512]{1,0:T(8,128)(2,1)} %param.21) | copy-start | bytes 196612
  332.8 532.7 %copy-start.1 = (bf16[64,4096]{1,0:T(8,128)(2,1)S(1)}, bf16[64,4096]{1,0:T(8,128)(2,1)}, u32[]{:S(2)}) copy-start(bf16[64,4096]{1,0:T(8,128)(2,1)} %param.16) | copy-start | bytes 1572868
  332.8 532.7 %copy-start.4 = (s32[64]{0:T(128)S(1)}, s32[64]{0:T(128)}, u32[]{:S(2)}) copy-start(s32[64]{0:T(128)} %param.17) | copy-start | bytes 772
  332.8 369.0 %all-reduce.2.cloned.1.call-start = ((), (), s32[]{:S(2)}) async-start(), calls=%async_computation.3 | async-start | bytes 262144 | tf_op jit(solution)/shard_map/psum | solution.py:78
  662.5 500.5 %all-gather.5.cloned.1.call-start = ((), (), s32[]{:S(2)}) async-start(), calls=%async_computation.4 | async-start | bytes 4259840 | tf_op jit(solution)/shard_map/all_gather | solution.py:84
  865.4 300.7 %copy-start.5 = (s32[64]{0:T(128)S(1)}, s32[64]{0:T(128)}, u32[]{:S(2)}) copy-start(s32[64]{0:T(128)} %param.18) | copy-start | bytes 772
Sparse Core Ops, SparseCore 0:
  9.8 306.4 all-gather.2
  332.9 329.4 reduce-scatter.1
  665.1 36.6 all-reduce.1
  865.5 297.4 all-gather.4
where the time goes:
time: 1170 us
  waiting for transfers between devices  951 us (81%)
  blocking collectives  160 us (14%)
  matrix products  32.9 us (3%)
  other arithmetic  15.1 us (1%)
  between operations  14.6 us (1%)
    reduce_scatter x1, waiting for transfers between devices, local(): lax.psum_scatter(outer_rows(gathered, all_scores), 'fsdp', scatter_dimens...  330 us
    all_gather x1, waiting for transfers between devices, local(): lax.all_gather(new_head, 'fsdp', axis=0, tiled=True)  294 us
    all_gather x1, waiting for transfers between devices, local(): lax.all_gather(head_weight, 'fsdp', axis=0, tiled=True)  288 us
    psum x1, blocking collectives, local(): squares = lax.psum(jnp.sum(grad_shard * grad_shard), 'fsdp')  160 us
    psum x1, waiting for transfers between devices, local(): grad_shard = lax.psum(grad_shard, 'grp')  39.2 us
  transfers between devices with their start and end apart: 4, of which 4 were waited for; matrix products, arithmetic and copies ran while one was open for 2% of the time, Pallas kernels for 0%

commit v1 on v0

--- a/solution.py
+++ b/solution.py
@@ -1,13 +1,23 @@
+import functools
+import itertools
+
 import jax
 import jax.numpy as jnp
 from jax import lax
+from jax.experimental import pallas as pl
+from jax.experimental.pallas import tpu as pltpu
 from jax.sharding import PartitionSpec as P
 
 ACTIONS = 512
 STATIONS = 512
 EPI_BLK = 8
 STEPS = 64
-
+D = 4096
+MESH = pl.DeviceIdType.MESH
+NY, NX, NZ = 4, 4, 8
+ROWS = 32
+HALF = 256
+PART = 128
 
 step_length = 8.0
 
@@ -45,6 +55,344 @@
     return lax.dot_general(
         left, right, (((0,), (0,)), ((), ())), preferred_element_type=jnp.float32
     )
+
+
+class Place:
+    def __init__(self):
+        grp, shard = lax.axis_index("grp"), lax.axis_index("fsdp")
+        self.core = lax.rem(grp, 2)
+        self.y = lax.div(grp, 2) * 2 + lax.div(shard, 32)
+        self.x = lax.rem(lax.div(shard, 8), 4)
+        self.z = lax.rem(shard, 8)
+        self.y_hi = lax.div(grp, 2)
+        self.shard = shard
+
+    def at(self, y=None, x=None, z=None, core=None):
+        y = self.y if y is None else y
+        x = self.x if x is None else x
+        z = self.z if z is None else z
+        core = self.core if core is None else core
+        return (lax.div(y, 2) * 2 + core, lax.rem(y, 2) * 32 + x * 8 + z)
+
+    def sibling(self):
+        return self.at(core=1 - self.core)
+
+    def along_z(self, k):
+        return self.at(z=lax.rem(self.z + k, NZ))
+
+    def along_y(self, k):
+        return self.at(y=lax.rem(self.y + k, NY))
+
+    def along_x(self, k):
+        return self.at(x=lax.rem(self.x + k, NX))
+
+
+def greet(here):
+    barrier = pltpu.get_barrier_semaphore()
+    friends = [here.along_z(k) for k in range(1, NZ)]
+    friends += [here.along_y(1), here.along_y(3), here.along_x(1), here.along_x(3)]
+    friends += [here.sibling()]
+    for friend in friends:
+        pl.semaphore_signal(barrier, inc=1, device_id=friend, device_id_type=MESH)
+    pl.semaphore_wait(barrier, len(friends))
+
+
+def send(src, dst, sems, index, device):
+    copy = pltpu.make_async_remote_copy(
+        src_ref=src,
+        dst_ref=dst,
+        send_sem=sems[0].at[index],
+        recv_sem=sems[1].at[index],
+        device_id=device,
+        device_id_type=MESH,
+    )
+    copy.start()
+    return copy
+
+
+def together(*walks):
+    for _ in itertools.zip_longest(*walks):
+        pass
+
+
+GATHER_SEMS = 7 + 6 + 6 + 8
+
+
+def gather_part(buf, first, second, along_first, along_second, here, sems, base):
+    core, z = here.core, here.z
+    sends = []
+    mine = buf.at[core, second, first, z]
+    for k in range(1, NZ):
+        sends.append(send(mine, mine, sems, base + k - 1, here.along_z(k)))
+    yield
+    for copy in sends[-7:]:
+        copy.wait_recv()
+    base += 7
+
+    def ring(view, me, along, base, arrived):
+        plus, minus = along(1), along(3)
+        after, opposite, before = lax.rem(me + 1, 4), lax.rem(me + 2, 4), lax.rem(me + 3, 4)
+        h0, h1 = view(me, 0), view(me, 1)
+        c = [
+            send(h0, h0, sems, base + 0, plus),
+            send(h1, h1, sems, base + 1, minus),
+            send(h1, h1, sems, base + 2, plus),
+            send(h0, h0, sems, base + 3, minus),
+        ]
+        arrived(me, 0)
+        arrived(me, 1)
+        yield
+        c[0].wait_recv()
+        onward = view(before, 0)
+        c.append(send(onward, onward, sems, base + 4, plus))
+        arrived(before, 0)
+        yield
+        c[1].wait_recv()
+        onward = view(after, 1)
+        c.append(send(onward, onward, sems, base + 5, minus))
+        arrived(after, 1)
+        yield
+        c[2].wait_recv()
+        arrived(before, 1)
+        yield
+        c[3].wait_recv()
+        arrived(after, 0)
+        yield
+        c[4].wait_recv()
+        arrived(opposite, 0)
+        yield
+        c[5].wait_recv()
+        arrived(opposite, 1)
+        sends.extend(c)
+
+    yield from ring(
+        lambda b, h: buf.at[core, second, b, pl.ds(4 * h, 4)],
+        first,
+        along_first,
+        base,
+        lambda b, h: None,
+    )
+    base += 6
+    outer = lambda b, h: buf.at[core, b, pl.ds(2 * h, 2)]
+    shared = []
+
+    def share(b, h):
+        shared.append(
+            send(outer(b, h), outer(b, h), sems, base + 6 + len(shared), here.sibling())
+        )
+
+    yield from ring(outer, second, along_second, base, share)
+    yield
+    for copy in shared:
+        copy.wait_recv()
+    for copy in sends + shared:
+        copy.wait_send()
+
+
+def gather(buf_a, buf_b, here, sems):
+    together(
+        gather_part(buf_a, here.x, here.y, here.along_x, here.along_y, here, sems, 0),
+        gather_part(buf_b, here.y, here.x, here.along_y, here.along_x, here, sems, GATHER_SEMS),
+    )
+
+
+SUM_SEMS = 6 + 6 + 7
+
+
+def sum_part(total, outer, inner, along_outer, along_inner, bufs, here, sems, base):
+    out1, in1, out2, in2, out3, in3 = bufs
+    sends = []
+
+    def ring(block, me, along, out, come, base):
+        plus, minus = along(1), along(3)
+        after, opposite, before = lax.rem(me + 1, 4), lax.rem(me + 2, 4), lax.rem(me + 3, 4)
+
+        def post(slot, value, device):
+            out[slot] = value.astype(jnp.bfloat16)
+            copy = send(out.at[slot], come.at[slot], sems, base + slot, device)
+            sends.append(copy)
+            return copy
+
+        def got(slot):
+            return come[slot].astype(jnp.float32)
+
+        c0 = post(0, block(opposite, 0)[...], plus)
+        c1 = post(1, block(opposite, 1)[...], minus)
+        c2 = post(2, block(after, 1)[...], plus)
+        c3 = post(3, block(before, 0)[...], minus)
+        yield
+        c0.wait_recv()
+        c4 = post(4, block(after, 0)[...] + got(0), plus)
+        yield
+        c1.wait_recv()
+        c5 = post(5, block(before, 1)[...] + got(1), minus)
+        yield
+        c2.wait_recv()
+        c3.wait_recv()
+        low, high = block(me, 0), block(me, 1)
+        low[...] = low[...] + got(3)
+        high[...] = high[...] + got(2)
+        yield
+        c4.wait_recv()
+        low[...] = low[...] + got(4)
+        yield
+        c5.wait_recv()
+        high[...] = high[...] + got(5)
+
+    yield from ring(
+        lambda b, h: total.at[b, pl.ds(2 * h, 2)], outer, along_outer, out1, in1, base
+    )
+    base += 6
+    yield from ring(
+        lambda b, h: total.at[outer, b, pl.ds(4 * h, 4)], inner, along_inner, out2, in2, base
+    )
+    base += 6
+    last = []
+    for k in range(1, NZ):
+        peer = lax.rem(here.z + k, NZ)
+        out3[k - 1] = total[outer, inner, peer].astype(jnp.bfloat16)
+        last.append(
+            send(out3.at[k - 1], in3.at[k - 1], sems, base + k - 1, here.along_z(k))
+        )
+    yield
+    for copy in last:
+        copy.wait_recv()
+    result = total[outer, inner, here.z]
+    for k in range(1, NZ):
+        result = result + in3[k - 1].astype(jnp.float32)
+    total[outer, inner, here.z] = result
+    for copy in sends + last:
+        copy.wait_send()
+
+
+def head_kernel(shard_ref, whole_ref, buf_a, buf_b, send_sems, recv_sems):
+    here = Place()
+    rows = pl.ds(pl.multiple_of(here.y_hi * ROWS, ROWS), ROWS)
+    for part, (buf, spot) in enumerate(((buf_a, (here.y, here.x)), (buf_b, (here.x, here.y)))):
+        cols = pl.ds(pl.multiple_of(here.core * HALF + part * PART, PART), PART)
+        buf[here.core, spot[0], spot[1], here.z] = shard_ref[rows, cols]
+    greet(here)
+    gather(buf_a, buf_b, here, (send_sems, recv_sems))
+    for core, y, x in itertools.product(range(2), range(NY), range(NX)):
+        for part, blocks in enumerate((buf_a[core, y, x], buf_b[core, x, y])):
+            cols = pl.ds(core * HALF + part * PART, PART)
+            whole_ref[y % 2, x, :, y // 2, :, cols] = blocks
+
+
+def part_buffers():
+    bf = jnp.bfloat16
+    return [
+        pltpu.VMEM((6, 2, NZ, ROWS, PART), bf),
+        pltpu.VMEM((6, 2, NZ, ROWS, PART), bf),
+        pltpu.VMEM((6, 4, ROWS, PART), bf),
+        pltpu.VMEM((6, 4, ROWS, PART), bf),
+        pltpu.VMEM((NZ - 1, ROWS, PART), bf),
+        pltpu.VMEM((NZ - 1, ROWS, PART), bf),
+    ]
+
+
+def step_kernel(grad_hbm, head_ref, new_ref, grad, out0, in0, total_a, total_b, *rest):
+    bufs_a, bufs_b = rest[:6], rest[6:12]
+    buf_a, buf_b = rest[12:14]
+    load_sem, pair_send, pair_recv, sum_send, sum_recv, all_send, all_recv = rest[14:]
+    here = Place()
+    load = pltpu.make_async_copy(grad_hbm, grad, load_sem)
+    load.start()
+    greet(here)
+    load.wait()
+    own = pl.ds(pl.multiple_of(here.core * HALF, HALF), HALF)
+    other = pl.ds(pl.multiple_of((1 - here.core) * HALF, HALF), HALF)
+    pairs = []
+    for k in range(8):
+        rows = pl.ds(512 * k, 512)
+        out0[k] = grad[rows, other].astype(jnp.bfloat16)
+        pairs.append(send(out0.at[k], in0.at[k], (pair_send, pair_recv), k, here.sibling()))
+    for k in range(8):
+        pairs[k].wait_recv()
+        y_lo, x = k // 4, k % 4
+        both = grad[pl.ds(512 * k, 512), own] + in0[k].astype(jnp.float32)
+        both = both.reshape(NZ, 2, ROWS, HALF)
+        for y_hi in range(2):
+            y = 2 * y_hi + y_lo
+            total_a[y, x] = both[:, y_hi, :, :PART]
+            total_b[x, y] = both[:, y_hi, :, PART:]
+    sems = (sum_send, sum_recv)
+    together(
+        sum_part(total_a, here.y, here.x, here.along_y, here.along_x, bufs_a, here, sems, 0),
+        sum_part(
+            total_b, here.x, here.y, here.along_x, here.along_y, bufs_b, here, sems, SUM_SEMS
+        ),
+    )
+    buf_a[here.core, here.y, here.x, here.z] = total_a[here.y, here.x, here.z].astype(jnp.bfloat16)
+    buf_b[here.core, here.x, here.y, here.z] = total_b[here.x, here.y, here.z].astype(jnp.bfloat16)
+    gather(buf_a, buf_b, here, (all_send, all_recv))
+    for copy in pairs:
+        copy.wait_send()
+    squares = jnp.zeros((ROWS, PART), jnp.float32)
+    for core, y, x in itertools.product(range(2), range(NY), range(NX)):
+        for block in (buf_a[core, y, x], buf_b[core, x, y]):
+            block = block.astype(jnp.float32)
+            squares = squares + jnp.sum(block * block, axis=0)
+    scale = step_length * lax.rsqrt(jnp.sum(squares, keepdims=True) + 1e-06)
+    for core, y, x in itertools.product(range(2), range(NY), range(NX)):
+        for part, block in enumerate((buf_a[core, y, x], buf_b[core, x, y])):
+            cols = pl.ds(core * HALF + part * PART, PART)
+            head = head_ref[y % 2, x, :, y // 2, :, cols].astype(jnp.float32)
+            step = block.astype(jnp.float32) * scale.reshape(1, 1, 1)
+            new_ref[y % 2, x, :, y // 2, :, cols] = (head - step).astype(jnp.bfloat16)
+
+
+SPREAD = (2, NX, NZ, 2, ROWS, ACTIONS)
+
+
+def dma_sems(count):
+    return [pltpu.SemaphoreType.DMA((count,)), pltpu.SemaphoreType.DMA((count,))]
+
+
+def gather_buffers():
+    return [
+        pltpu.VMEM((2, NY, NX, NZ, ROWS, PART), jnp.bfloat16),
+        pltpu.VMEM((2, NX, NY, NZ, ROWS, PART), jnp.bfloat16),
+    ]
+
+
+def gather_head(shard):
+    return pl.pallas_call(
+        head_kernel,
+        out_shape=jax.ShapeDtypeStruct(SPREAD, jnp.bfloat16),
+        in_specs=[pl.BlockSpec(memory_space=pltpu.VMEM)],
+        out_specs=pl.BlockSpec(memory_space=pltpu.VMEM),
+        scratch_shapes=gather_buffers() + dma_sems(2 * GATHER_SEMS),
+        compiler_params=pltpu.CompilerParams(
+            collective_id=0, has_side_effects=True, vmem_limit_bytes=32 << 20
+        ),
+    )(shard)
+
+
+def take_step(grad, head):
+    return pl.pallas_call(
+        step_kernel,
+        out_shape=jax.ShapeDtypeStruct(SPREAD, jnp.bfloat16),
+        in_specs=[pl.BlockSpec(memory_space=pl.ANY), pl.BlockSpec(memory_space=pltpu.VMEM)],
+        out_specs=pl.BlockSpec(memory_space=pltpu.VMEM),
+        scratch_shapes=[
+            pltpu.VMEM((D, ACTIONS), jnp.float32),
+            pltpu.VMEM((8, 512, HALF), jnp.bfloat16),
+            pltpu.VMEM((8, 512, HALF), jnp.bfloat16),
+            pltpu.VMEM((NY, NX, NZ, ROWS, PART), jnp.float32),
+            pltpu.VMEM((NX, NY, NZ, ROWS, PART), jnp.float32),
+            *part_buffers(),
+            *part_buffers(),
+            *gather_buffers(),
+            pltpu.SemaphoreType.DMA(()),
+            *dma_sems(8),
+            *dma_sems(2 * SUM_SEMS),
+            *dma_sems(2 * GATHER_SEMS),
+        ],
+        compiler_params=pltpu.CompilerParams(
+            collective_id=1, has_side_effects=True, vmem_limit_bytes=56 << 20
+        ),
+    )(grad, head)
 
 
 def local(
@@ -60,10 +408,11 @@
     norm_gain,
     head_weight,
 ):
+    head = gather_head(head_weight)
     features = station_rows(traj_hidden, traj_tokens, station_table, norm_gain)
     rollout = station_rows(roll_hidden, roll_tokens, station_table, norm_gain)
     advantage = episode_advantage(traj_return, traj_episode[0])
-    logits = add_columns(features, lax.all_gather(head_weight, "fsdp", axis=0, tiled=True))
+    logits = add_columns(features, head.reshape(D, ACTIONS))
     top = jnp.max(logits, axis=-1, keepdims=True)
     expo = jnp.exp(logits - top)
     probs = expo / jnp.sum(expo, axis=-1, keepdims=True)
@@ -71,17 +420,9 @@
         jnp.float32
     )
     scores = (advantage[:, None] * (probs - chosen)).astype(jnp.bfloat16)
-    gathered, all_scores = (features, scores)
-    grad_shard = lax.psum_scatter(
-        outer_rows(gathered, all_scores), "fsdp", scatter_dimension=0, tiled=True
-    )
-    grad_shard = lax.psum(grad_shard, "grp")
-    squares = lax.psum(jnp.sum(grad_shard * grad_shard), "fsdp")
-    gnorm = jnp.sqrt(squares + 1e-06)
-    new_head = (head_weight.astype(jnp.float32) - step_length * grad_shard / gnorm).astype(
-        jnp.bfloat16
-    )
-    roll_logits = add_columns(rollout, lax.all_gather(new_head, "fsdp", axis=0, tiled=True))
+    new_whole = take_step(outer_rows(features, scores), head).reshape(D, ACTIONS)
+    new_head = lax.dynamic_slice_in_dim(new_whole, lax.axis_index("fsdp") * 64, 64, axis=0)
+    roll_logits = add_columns(rollout, new_whole)
     action_logp = picked_logp(roll_logits, roll_action)
     episode_logp = jnp.sum(action_logp.reshape(-1, STEPS), axis=1)
     return (new_head, action_logp, episode_logp)

time: 1170 us -> 141 us (0.12)
  the two profiles are of different devices: /device:TPU:16 before, /device:TPU:1 now
where the time goes in v1:
time: 141 us; the launch traced here: 140 us
  Pallas kernels  98.9 us (70%)
  matrix products  27.4 us (19%)
  other arithmetic  10.7 us (8%)
  local copies, waits for them, and re-layouts  2.64 us (2%)
    pallas_call x1, Pallas kernels, take_step(): pl.pallas_call(step_kernel, out_shape=jax.ShapeDtypeStruct(SPREAD, jnp.bf...  63.2 us
    pallas_call x1, Pallas kernels, gather_head(): pl.pallas_call(head_kernel, out_shape=jax.ShapeDtypeStruct(SPREAD, jnp.bf...  35.7 us
    dot_general x2, matrix products, station_rows(): embedded = jnp.dot(lookup, table, preferred_element_type=jnp.float32)  9.82 us
    dot_general x2, matrix products, add_columns(): return jnp.dot(left, piece, preferred_element_type=jnp.float32)  9.6 us
    convert_element_type x1, other arithmetic, station_rows(): return (mixed * lax.rsqrt(power + 1e-05) * gain).astype(jnp.bfloat16)  8.89 us
    dot_general x1, matrix products, outer_rows(): lax.dot_general(left, right, (((0,), (0,)), ((), ())), preferred_element_...  7.68 us

profile of v1, /device:TPU:1, one launch (start us, length us, event | category | flops | bytes accessed | tf_op | source)
XLA Modules:
  0.0 140.5 jit_solution(15756229014534307353)
XLA Ops:
  0.6 0.0 copy-start.5
  0.6 8.8 %multiply_reduce_fusion = (f32[1024]{0:T(1024)S(1)}, f32[1024,4096]{1,0:T(8,128)S(1)}) fusion(bf16[1024,4096]{1,0:T(8,128)(2,1)} %param.11, bf16[512,4096]{1,0:T(8,128)(2,1)} %param.19, s32[1024]{0:T(1024)} %param.12), kind=kOutput, calls=%fused_computation.1 | convolution fusion | flops 4312267776 | bytes 29368320 | tf_op jit(solution)/shard_map/dot_general | solution.py:29
  9.5 0.0 copy-start.1
  9.5 8.9 %multiply_convert_fusion = bf16[1024,4096]{1,0:T(8,128)(2,1)} fusion(f32[1024,4096]{1,0:T(8,128)S(1)} %get-tuple-element.8, bf16[1024,4096]{1,0:T(8,128)(2,1)} %param.11, f32[4096]{0:T(1024)S(1)} %copy-done.5, f32[1024]{0:T(1024)S(1)} %add_rsqrt_fusion), kind=kLoop, calls=%fused_computation | loop fusion | flops 20971520 | bytes 33574912 | tf_op jit(solution)/shard_map/convert_element_type | solution.py:32
  18.4 35.7 %shard_map.130.head_ref = bf16[2,4,8,2,32,512]{5,4,3,2,1,0:T(8,128)(2,1)S(1)} custom-call(bf16[64,512]{1,0:T(8,128)(2,1)S(1)} %copy-done.1), custom_call_target="tpu_custom_call" | custom-call | tf_op jit(solution)/shard_map/pallas_call | solution.py:360
  54.1 0.0 copy-start
  54.1 0.0 copy-start.7
  54.1 0.0 copy-start.6
  54.1 0.0 slice-start.1
  54.1 0.0 copy-start.10
  54.1 8.6 %fusion.18 = (f32[1024]{0:T(1024)S(1)}, f32[1024,512]{0,1:T(8,128)S(1)}) fusion(bf16[1024,4096]{1,0:T(8,128)(2,1)} %multiply_convert_fusion, bf16[4096,512]{1,0:T(8,128)(2,1)S(1)} %bitcast.22), kind=kOutput, calls=%fused_computation.40 | convolution fusion | flops 4295490560 | bytes 14684160 | tf_op jit(solution)/shard_map/dot_general | solution.py:36
  62.8 0.3 fusion.1
  63.1 0.1 convert_reduce_fusion
  63.2 0.1 fusion.3
  63.3 0.2 fusion.14
  63.6 7.7 %fusion.4.grad_hbm = f32[4096,512]{1,0:T(8,128)} fusion(bf16[1024,4096]{1,0:T(8,128)(2,1)S(1)} %bitcast.26, f32[1024,512]{0,1:T(8,128)S(1)} %get-tuple-element.10, s32[1024]{0:T(1024)S(1)} %copy-done.10, f32[1024]{0:T(1024)S(1)} %fusion.1, f32[1024]{0:T(1024)S(1)} %get-tuple-element.9, f32[1024]{0:T(1024)S(1)} %sub.27), kind=kOutput, calls=%fused_computation.13 | convolution fusion | flops 4298637312 | bytes 18890752 | tf_op jit(solution)/shard_map/dot_general | solution.py:55
  71.3 63.2 %shard_map.131 = bf16[2,4,8,2,32,512]{5,4,3,2,1,0:T(8,128)(2,1)} custom-call(f32[4096,512]{1,0:T(8,128)} %fusion.4.grad_hbm, bf16[2,4,8,2,32,512]{5,4,3,2,1,0:T(8,128)(2,1)} %copy-done), custom_call_target="tpu_custom_call" | custom-call | tf_op jit(solution)/shard_map/pallas_call | solution.py:373
  134.5 0.0 copy-start.9
  134.5 1.0 multiply_reduce_fusion.1
  135.6 1.1 copy-done.2
  136.7 1.0 fusion.19
  137.7 0.2 exponential_reduce_fusion
  137.9 1.1 fusion.17
  139.0 1.5 %constant_dynamic-slice_fusion = bf16[64,512]{1,0:T(8,128)(2,1)} fusion(bf16[4096,512]{1,0:T(8,128)(2,1)} %bitcast.23, s32[]{:T(128)S(6)} %select_n.3), kind=kLoop, calls=%fused_computation.38 | loop fusion | bytes 131076 | tf_op jit(solution)/shard_map/dynamic_slice | solution.py:424
  (21 shorter events, 0.1 us)
Async XLA Ops:
  0.6 8.8 %copy-start.5 = (f32[4096]{0:T(1024)S(1)}, f32[4096]{0:T(1024)}, u32[]{:S(2)}) copy-start(f32[4096]{0:T(1024)} %param.20) | copy-start | bytes 49156
  9.5 8.9 %copy-start.1 = (bf16[64,512]{1,0:T(8,128)(2,1)S(1)}, bf16[64,512]{1,0:T(8,128)(2,1)}, u32[]{:S(2)}) copy-start(bf16[64,512]{1,0:T(8,128)(2,1)} %shard_ref.1) | copy-start | bytes 196612
  18.4 45.2 %slice-start = ((s8[8388608]{0:T(1024)(128)(4,1)}), s8[4194304]{0:T(1024)(128)(4,1)S(1)}, s32[]{:S(2)}) async-start(s8[8388608]{0:T(1024)(128)(4,1)} %bitcast.25), calls=%async_computation | async-start | bytes 8388608
  54.1 8.7 %copy-start = (bf16[2,4,8,2,32,512]{5,4,3,2,1,0:T(8,128)(2,1)}, bf16[2,4,8,2,32,512]{5,4,3,2,1,0:T(8,128)(2,1)S(1)}, u32[]{:S(2)}) copy-start(bf16[2,4,8,2,32,512]{5,4,3,2,1,0:T(8,128)(2,1)S(1)} %shard_map.130.head_ref) | copy-start | bytes 12582916
  54.1 9.0 %copy-start.7 = (s32[1,1024]{1,0:T(1,128)S(1)}, s32[1,1024]{1,0:T(1,128)}, u32[]{:S(2)}) copy-start(s32[1,1024]{1,0:T(1,128)} %param.15) | copy-start | bytes 12292
  54.1 9.1 %copy-start.6 = (f32[1024]{0:T(1024)S(1)}, f32[1024]{0:T(1024)}, u32[]{:S(2)}) copy-start(f32[1024]{0:T(1024)} %param.14) | copy-start | bytes 12292
  54.1 9.4 %slice-start.1 = ((s8[8388608]{0:T(1024)(128)(4,1)}), s8[4194304]{0:T(1024)(128)(4,1)S(1)}, s32[]{:S(2)}) async-start(s8[8388608]{0:T(1024)(128)(4,1)} %bitcast.25), calls=%async_computation.1 | async-start | bytes 8388608
  54.1 9.4 %copy-start.10 = (s32[1024]{0:T(1024)S(1)}, s32[1024]{0:T(1024)}, u32[]{:S(2)}) copy-start(s32[1024]{0:T(1024)} %param.13) | copy-start | bytes 12292
  71.2 63.2 %copy-start.3 = (bf16[512,4096]{1,0:T(8,128)(2,1)S(1)}, bf16[512,4096]{1,0:T(8,128)(2,1)}, u32[]{:S(2)}) copy-start(bf16[512,4096]{1,0:T(8,128)(2,1)} %param.19) | copy-start | bytes 12582916
  71.2 63.2 %copy-start.4 = (bf16[64,4096]{1,0:T(8,128)(2,1)S(1)}, bf16[64,4096]{1,0:T(8,128)(2,1)}, u32[]{:S(2)}) copy-start(bf16[64,4096]{1,0:T(8,128)(2,1)} %param.16) | copy-start | bytes 1572868
  71.3 63.3 %copy-start.8 = (s32[64]{0:T(128)S(1)}, s32[64]{0:T(128)}, u32[]{:S(2)}) copy-start(s32[64]{0:T(128)} %param.17) | copy-start | bytes 772
  134.5 2.2 %copy-start.2 = (bf16[2,4,8,2,32,512]{5,4,3,2,1,0:T(8,128)(2,1)S(1)}, bf16[2,4,8,2,32,512]{5,4,3,2,1,0:T(8,128)(2,1)}, u32[]{:S(2)}) copy-start(bf16[2,4,8,2,32,512]{5,4,3,2,1,0:T(8,128)(2,1)} %shard_map.131) | copy-start | bytes 12582916
  134.5 3.1 %copy-start.9 = (s32[64]{0:T(128)S(1)}, s32[64]{0:T(128)}, u32[]{:S(2)}) copy-start(s32[64]{0:T(128)} %param.18) | copy-start | bytes 772

commit v2 on v1

--- a/solution.py
+++ b/solution.py
@@ -1,4 +1,3 @@
-import functools
 import itertools
 
 import jax
@@ -20,41 +19,6 @@
 PART = 128
 
 step_length = 8.0
-
-
-def station_rows(hidden, tokens, table, gain):
-    lookup = (tokens[:, None] == jnp.arange(STATIONS, dtype=jnp.int32)[None, :]).astype(
-        jnp.bfloat16
-    )
-    embedded = jnp.dot(lookup, table, preferred_element_type=jnp.float32)
-    mixed = hidden.astype(jnp.float32) + embedded
-    power = jnp.mean(mixed * mixed, axis=-1, keepdims=True)
-    return (mixed * lax.rsqrt(power + 1e-05) * gain).astype(jnp.bfloat16)
-
-
-def add_columns(left, piece):
-    return jnp.dot(left, piece, preferred_element_type=jnp.float32)
-
-
-def picked_logp(logits, actions):
-    top = jnp.max(logits, axis=-1, keepdims=True)
-    total = jnp.log(jnp.sum(jnp.exp(logits - top), axis=-1)) + top[:, 0]
-    chosen = (actions[:, None] == jnp.arange(ACTIONS, dtype=jnp.int32)[None, :]).astype(jnp.float32)
-    return jnp.sum(logits * chosen, axis=-1) - total
-
-
-def episode_advantage(returns, episode):
-    member = (episode[:, None] == jnp.arange(EPI_BLK, dtype=jnp.int32)[None, :]).astype(jnp.float32)
-    sums = jnp.dot(member.T, returns, precision=lax.Precision.HIGHEST)
-    counts = jnp.sum(member, axis=0)
-    baseline = jnp.dot(member, sums / counts, precision=lax.Precision.HIGHEST)
-    return returns - baseline
-
-
-def outer_rows(left, right):
-    return lax.dot_general(
-        left, right, (((0,), (0,)), ((), ())), preferred_element_type=jnp.float32
-    )
 
 
 class Place:
@@ -189,8 +153,8 @@
         copy.wait_send()
 
 
-def gather(buf_a, buf_b, here, sems):
-    together(
+def gather_walk(buf_a, buf_b, here, sems):
+    return itertools.zip_longest(
         gather_part(buf_a, here.x, here.y, here.along_x, here.along_y, here, sems, 0),
         gather_part(buf_b, here.y, here.x, here.along_y, here.along_x, here, sems, GATHER_SEMS),
     )
@@ -265,20 +229,6 @@
         copy.wait_send()
 
 
-def head_kernel(shard_ref, whole_ref, buf_a, buf_b, send_sems, recv_sems):
-    here = Place()
-    rows = pl.ds(pl.multiple_of(here.y_hi * ROWS, ROWS), ROWS)
-    for part, (buf, spot) in enumerate(((buf_a, (here.y, here.x)), (buf_b, (here.x, here.y)))):
-        cols = pl.ds(pl.multiple_of(here.core * HALF + part * PART, PART), PART)
-        buf[here.core, spot[0], spot[1], here.z] = shard_ref[rows, cols]
-    greet(here)
-    gather(buf_a, buf_b, here, (send_sems, recv_sems))
-    for core, y, x in itertools.product(range(2), range(NY), range(NX)):
-        for part, blocks in enumerate((buf_a[core, y, x], buf_b[core, x, y])):
-            cols = pl.ds(core * HALF + part * PART, PART)
-            whole_ref[y % 2, x, :, y // 2, :, cols] = blocks
-
-
 def part_buffers():
     bf = jnp.bfloat16
     return [
@@ -291,31 +241,151 @@
     ]
 
 
-def step_kernel(grad_hbm, head_ref, new_ref, grad, out0, in0, total_a, total_b, *rest):
+TILE = 256
+WIDE = 1024
+
+
+def one_hot(column, count):
+    spots = lax.broadcasted_iota(jnp.int32, (column.shape[0], count), 1).astype(jnp.float32)
+    return column == spots
+
+
+def columns_of(rows):
+    return jnp.transpose(rows)
+
+
+def advantage_of(returns, episode):
+    baseline = jnp.zeros_like(returns)
+    for number in range(EPI_BLK):
+        member = (episode == number).astype(jnp.float32)
+        total = jnp.sum(returns * member, keepdims=True)
+        count = jnp.sum(member, keepdims=True)
+        baseline = baseline + member * (total / count)
+    return returns - baseline
+
+
+def station_rows(rows_ref, tokens, table, gain, mixed, step):
+    n = rows_ref.shape[0]
+    lookup = one_hot(tokens, STATIONS).astype(jnp.bfloat16)
+    power = jnp.zeros((n, 1), jnp.float32)
+    for left in range(0, D, WIDE):
+        cols = pl.ds(left, WIDE)
+        value = rows_ref[:, cols].astype(jnp.float32) + jnp.dot(
+            lookup, table[:, cols], preferred_element_type=jnp.float32
+        )
+        mixed[:n, cols] = value
+        power = power + jnp.sum(value * value, axis=-1, keepdims=True)
+        step()
+    inverse = lax.rsqrt(power * (1.0 / D) + 1e-05)
+    for left in range(0, D, WIDE):
+        cols = pl.ds(left, WIDE)
+        rows_ref[:, cols] = (mixed[:n, cols] * inverse * gain[:, cols]).astype(jnp.bfloat16)
+    step()
+
+
+def whole_kernel(
+    hidden_hbm,
+    roll_hbm,
+    table_hbm,
+    gain,
+    ints,
+    returns,
+    episode,
+    shard,
+    new_ref,
+    logp_ref,
+    episode_ref,
+    features,
+    rollout,
+    table,
+    mixed,
+    scores,
+    head,
+    out0,
+    in0,
+    total_a,
+    total_b,
+    *rest,
+):
     bufs_a, bufs_b = rest[:6], rest[6:12]
-    buf_a, buf_b = rest[12:14]
-    load_sem, pair_send, pair_recv, sum_send, sum_recv, all_send, all_recv = rest[14:]
+    head_a, head_b, buf_a, buf_b = rest[12:16]
+    load_sem, pair_send, pair_recv, sum_send, sum_recv = rest[16:21]
+    head_send, head_recv, all_send, all_recv = rest[21:]
     here = Place()
-    load = pltpu.make_async_copy(grad_hbm, grad, load_sem)
-    load.start()
+
+    loads = [pltpu.make_async_copy(table_hbm, table, load_sem.at[0])]
+    tiles = [pl.ds(TILE * i, TILE) for i in range(4)]
+    for i, rows in enumerate(tiles):
+        loads.append(
+            pltpu.make_async_copy(hidden_hbm.at[rows], features.at[rows], load_sem.at[1 + i])
+        )
+    loads.append(pltpu.make_async_copy(roll_hbm, rollout, load_sem.at[5]))
+    for load in loads:
+        load.start()
+
+    rows = pl.ds(pl.multiple_of(here.y_hi * ROWS, ROWS), ROWS)
+    for part, (buf, spot) in enumerate(((head_a, (here.y, here.x)), (head_b, (here.x, here.y)))):
+        cols = pl.ds(pl.multiple_of(here.core * HALF + part * PART, PART), PART)
+        buf[here.core, spot[0], spot[1], here.z] = shard[rows, cols]
     greet(here)
-    load.wait()
-    own = pl.ds(pl.multiple_of(here.core * HALF, HALF), HALF)
-    other = pl.ds(pl.multiple_of((1 - here.core) * HALF, HALF), HALF)
+    walk = gather_walk(head_a, head_b, here, (head_send, head_recv))
+    next(walk)
+    turn = itertools.count(1)
+
+    def step():
+        if next(turn) % 2 == 0:
+            next(walk, None)
+
+    numbers = columns_of(ints[...].astype(jnp.float32))
+    advantage = columns_of(advantage_of(returns[...], episode[...]))
+
+    def column(values, first, tile):
+        return jnp.concatenate([values[:, first + 2 * tile + j][:, None] for j in range(2)], axis=0)
+
+    loads[0].wait()
+    for i, rows in enumerate(tiles):
+        loads[1 + i].wait()
+        station_rows(features.at[rows], column(numbers, 0, i), table, gain, mixed, step)
+    loads[5].wait()
+    station_rows(rollout, numbers[:64, 16:17], table, gain, mixed, step)
+    for _ in walk:
+        pass
+    for core, y, x in itertools.product(range(2), range(NY), range(NX)):
+        for part, blocks in enumerate((head_a[core, y, x], head_b[core, x, y])):
+            head[y % 2, x, :, y // 2, :, pl.ds(core * HALF + part * PART, PART)] = blocks
+
+    for i, rows in enumerate(tiles):
+        logits = jnp.dot(
+            features[rows, :],
+            head[...].reshape(D, ACTIONS),
+            preferred_element_type=jnp.float32,
+        )
+        expo = jnp.exp(logits - jnp.max(logits, axis=-1, keepdims=True))
+        probs = expo / jnp.sum(expo, axis=-1, keepdims=True)
+        chosen = one_hot(column(numbers, 8, i), ACTIONS).astype(jnp.float32)
+        value = (column(advantage, 0, i) * (probs - chosen)).astype(jnp.bfloat16)
+        scores[0, rows] = value[:, :HALF]
+        scores[1, rows] = value[:, HALF:]
+
     pairs = []
+    mine, theirs = scores[here.core], scores[1 - here.core]
     for k in range(8):
-        rows = pl.ds(512 * k, 512)
-        out0[k] = grad[rows, other].astype(jnp.bfloat16)
+        left = jnp.transpose(features[:, pl.ds(512 * k, 512)])
+        out0[k] = jnp.dot(left, theirs, preferred_element_type=jnp.float32).astype(jnp.bfloat16)
         pairs.append(send(out0.at[k], in0.at[k], (pair_send, pair_recv), k, here.sibling()))
+        own = jnp.dot(left, mine, preferred_element_type=jnp.float32).reshape(NZ, 2, ROWS, HALF)
+        for y_hi in range(2):
+            y, x = 2 * y_hi + k // 4, k % 4
+            total_a[y, x] = own[:, y_hi, :, :PART]
+            total_b[x, y] = own[:, y_hi, :, PART:]
     for k in range(8):
         pairs[k].wait_recv()
-        y_lo, x = k // 4, k % 4
-        both = grad[pl.ds(512 * k, 512), own] + in0[k].astype(jnp.float32)
-        both = both.reshape(NZ, 2, ROWS, HALF)
+        other = in0[k].astype(jnp.float32).reshape(NZ, 2, ROWS, HALF)
         for y_hi in range(2):
-            y = 2 * y_hi + y_lo
-            total_a[y, x] = both[:, y_hi, :, :PART]
-            total_b[x, y] = both[:, y_hi, :, PART:]
+            y, x = 2 * y_hi + k // 4, k % 4
+            total_a[y, x] = total_a[y, x] + other[:, y_hi, :, :PART]
+            total_b[x, y] = total_b[x, y] + other[:, y_hi, :, PART:]
+
     sems = (sum_send, sum_recv)
     together(
         sum_part(total_a, here.y, here.x, here.along_y, here.along_x, bufs_a, here, sems, 0),
@@ -325,9 +395,11 @@
     )
     buf_a[here.core, here.y, here.x, here.z] = total_a[here.y, here.x, here.z].astype(jnp.bfloat16)
     buf_b[here.core, here.x, here.y, here.z] = total_b[here.x, here.y, here.z].astype(jnp.bfloat16)
-    gather(buf_a, buf_b, here, (all_send, all_recv))
+    for _ in gather_walk(buf_a, buf_b, here, (all_send, all_recv)):
+        pass
     for copy in pairs:
         copy.wait_send()
+
     squares = jnp.zeros((ROWS, PART), jnp.float32)
     for core, y, x in itertools.product(range(2), range(NY), range(NX)):
         for block in (buf_a[core, y, x], buf_b[core, x, y]):
@@ -337,9 +409,19 @@
     for core, y, x in itertools.product(range(2), range(NY), range(NX)):
         for part, block in enumerate((buf_a[core, y, x], buf_b[core, x, y])):
             cols = pl.ds(core * HALF + part * PART, PART)
-            head = head_ref[y % 2, x, :, y // 2, :, cols].astype(jnp.float32)
-            step = block.astype(jnp.float32) * scale.reshape(1, 1, 1)
-            new_ref[y % 2, x, :, y // 2, :, cols] = (head - step).astype(jnp.bfloat16)
+            old = head[y % 2, x, :, y // 2, :, cols].astype(jnp.float32)
+            change = block.astype(jnp.float32) * scale.reshape(1, 1, 1)
+            head[y % 2, x, :, y // 2, :, cols] = (old - change).astype(jnp.bfloat16)
+    new_ref[...] = head[lax.rem(here.y, 2), here.x, here.z].reshape(2 * ROWS, ACTIONS)
+    logits = jnp.dot(
+        rollout[...], head[...].reshape(D, ACTIONS), preferred_element_type=jnp.float32
+    )
+    top = jnp.max(logits, axis=-1, keepdims=True)
+    total = jnp.log(jnp.sum(jnp.exp(logits - top), axis=-1, keepdims=True)) + top
+    chosen = one_hot(numbers[64:, 16:17], ACTIONS).astype(jnp.float32)
+    logp = jnp.sum(logits * chosen, axis=-1, keepdims=True) - total
+    logp_ref[...] = jnp.transpose(jnp.broadcast_to(logp, (STEPS, 128)))[:1, :]
+    episode_ref[...] = jnp.sum(logp, keepdims=True)
 
 
 SPREAD = (2, NX, NZ, 2, ROWS, ACTIONS)
@@ -356,27 +438,24 @@
     ]
 
 
-def gather_head(shard):
+def whole_step(hidden, roll, table, gain, ints, returns, episode, shard):
+    vmem, anywhere = pl.BlockSpec(memory_space=pltpu.VMEM), pl.BlockSpec(memory_space=pl.ANY)
     return pl.pallas_call(
-        head_kernel,
-        out_shape=jax.ShapeDtypeStruct(SPREAD, jnp.bfloat16),
-        in_specs=[pl.BlockSpec(memory_space=pltpu.VMEM)],
-        out_specs=pl.BlockSpec(memory_space=pltpu.VMEM),
-        scratch_shapes=gather_buffers() + dma_sems(2 * GATHER_SEMS),
-        compiler_params=pltpu.CompilerParams(
-            collective_id=0, has_side_effects=True, vmem_limit_bytes=32 << 20
+        whole_kernel,
+        out_shape=(
+            jax.ShapeDtypeStruct(shard.shape, jnp.bfloat16),
+            jax.ShapeDtypeStruct((1, STEPS), jnp.float32),
+            jax.ShapeDtypeStruct((1, 1), jnp.float32),
         ),
-    )(shard)
-
-
-def take_step(grad, head):
-    return pl.pallas_call(
-        step_kernel,
-        out_shape=jax.ShapeDtypeStruct(SPREAD, jnp.bfloat16),
-        in_specs=[pl.BlockSpec(memory_space=pl.ANY), pl.BlockSpec(memory_space=pltpu.VMEM)],
-        out_specs=pl.BlockSpec(memory_space=pltpu.VMEM),
+        in_specs=[anywhere] * 3 + [vmem] * 5,
+        out_specs=(vmem, vmem, vmem),
         scratch_shapes=[
-            pltpu.VMEM((D, ACTIONS), jnp.float32),
+            pltpu.VMEM((1024, D), jnp.bfloat16),
+            pltpu.VMEM((STEPS, D), jnp.bfloat16),
+            pltpu.VMEM((STATIONS, D), jnp.bfloat16),
+            pltpu.VMEM((TILE, D), jnp.float32),
+            pltpu.VMEM((2, 1024, HALF), jnp.bfloat16),
+            pltpu.VMEM(SPREAD, jnp.bfloat16),
             pltpu.VMEM((8, 512, HALF), jnp.bfloat16),
             pltpu.VMEM((8, 512, HALF), jnp.bfloat16),
             pltpu.VMEM((NY, NX, NZ, ROWS, PART), jnp.float32),
@@ -384,15 +463,17 @@
             *part_buffers(),
             *part_buffers(),
             *gather_buffers(),
-            pltpu.SemaphoreType.DMA(()),
+            *gather_buffers(),
+            pltpu.SemaphoreType.DMA((6,)),
             *dma_sems(8),
             *dma_sems(2 * SUM_SEMS),
             *dma_sems(2 * GATHER_SEMS),
+            *dma_sems(2 * GATHER_SEMS),
         ],
         compiler_params=pltpu.CompilerParams(
-            collective_id=1, has_side_effects=True, vmem_limit_bytes=56 << 20
+            collective_id=0, has_side_effects=True, vmem_limit_bytes=60 << 20
         ),
-    )(grad, head)
+    )(hidden, roll, table, gain, ints, returns, episode, shard)
 
 
 def local(
@@ -408,24 +489,19 @@
     norm_gain,
     head_weight,
 ):
-    head = gather_head(head_weight)
-    features = station_rows(traj_hidden, traj_tokens, station_table, norm_gain)
-    rollout = station_rows(roll_hidden, roll_tokens, station_table, norm_gain)
-    advantage = episode_advantage(traj_return, traj_episode[0])
-    logits = add_columns(features, head.reshape(D, ACTIONS))
-    top = jnp.max(logits, axis=-1, keepdims=True)
-    expo = jnp.exp(logits - top)
-    probs = expo / jnp.sum(expo, axis=-1, keepdims=True)
-    chosen = (traj_action[:, None] == jnp.arange(ACTIONS, dtype=jnp.int32)[None, :]).astype(
-        jnp.float32
-    )
-    scores = (advantage[:, None] * (probs - chosen)).astype(jnp.bfloat16)
-    new_whole = take_step(outer_rows(features, scores), head).reshape(D, ACTIONS)
-    new_head = lax.dynamic_slice_in_dim(new_whole, lax.axis_index("fsdp") * 64, 64, axis=0)
-    roll_logits = add_columns(rollout, new_whole)
-    action_logp = picked_logp(roll_logits, roll_action)
-    episode_logp = jnp.sum(action_logp.reshape(-1, STEPS), axis=1)
-    return (new_head, action_logp, episode_logp)
+    ints = jnp.concatenate([traj_tokens, traj_action, roll_tokens, roll_action]).reshape(17, 128)
+    ints = jnp.pad(ints, ((0, 7), (0, 0)))
+    new_head, action_logp, episode_logp = whole_step(
+        traj_hidden,
+        roll_hidden,
+        station_table,
+        norm_gain.reshape(1, D),
+        ints,
+        traj_return.reshape(8, 128),
+        traj_episode.reshape(8, 128),
+        head_weight,
+    )
+    return (new_head, action_logp.reshape(STEPS), episode_logp.reshape(1))
 
 
 def solution(mesh):

time: 141 us -> 109 us (0.77)
  matrix products: 27.4 us -> 0 us
  other arithmetic: 10.7 us -> 0 us
  Pallas kernels: 98.9 us -> 102 us
  between operations: 0.84 us -> 2.33 us
    dot_general x7 -> x0, matrix products: 27.4 us -> none  [the longest x2 9.82 us: station_rows(): embedded = jnp.dot(lookup, table, preferred_element_type=jnp.float32)]
    convert_element_type x1 -> x0, other arithmetic: 8.89 us -> none  [station_rows(): return (mixed * lax.rsqrt(power + 1e-05) * gain).astype(jnp.bfloat16)]
    pallas_call x2 -> x1, Pallas kernels: 98.9 us -> 102 us  [whole_step(): pl.pallas_call(whole_kernel, out_shape=(jax.ShapeDtypeStruct(shard.shape,...]
    reduce_sum x4 -> x0, other arithmetic: 1.79 us -> none  [the longest x1 1.13 us: local(): episode_logp = jnp.sum(action_logp.reshape(-1, STEPS), axis=1)]
    dynamic_slice x1 -> x0, local copies, waits for them, and re-layouts: 1.47 us -> none  [local(): lax.dynamic_slice_in_dim(new_whole, lax.axis_index('fsdp') * 64, 64, axis=0)]
    unnamed x26 -> x2, local copies, waits for them, and re-layouts: 1.17 us -> 2.59 us
where the time goes in v2:
time: 109 us
  Pallas kernels  102 us (94%)
  local copies, waits for them, and re-layouts  3.98 us (4%)
  between operations  2.33 us (2%)
    pallas_call x1, Pallas kernels, whole_step(): pl.pallas_call(whole_kernel, out_shape=(jax.ShapeDtypeStruct(shard.shape,...  102 us
    unnamed x2, local copies, waits for them, and re-layouts  2.59 us

profile of v2, /device:TPU:1, one launch (start us, length us, event | category | flops | bytes accessed | tf_op | source)
XLA Modules:
  0.0 108.6 jit_solution(15137956337084206141)
XLA Ops:
  0.6 0.8 concatenate.3
  1.4 0.6 pad.4.ints
  2.0 102.3 %shard_map.130 = (bf16[64,512]{1,0:T(8,128)(2,1)}, f32[1,64]{1,0:T(1,128)}, f32[1,1]{1,0:T(1,128)}) custom-call(bf16[1024,4096]{1,0:T(8,128)(2,1)} %hidden_hbm.1, bf16[64,4096]{1,0:T(8,128)(2,1)} %roll_hbm.1, bf16[512,4096]{1,0:T(8,128)(2,1)} %table_hbm.1, f32[1,4096]{1,0:T(1,128)} %bitcast.7, s32[24,128]{1,0:T(8,128)} %pad.4.ints, f32[8,128]{1,0:T(8,128)} %bitcast.8, ...), custom_call_target="tpu_custom_call" | custom-call | tf_op jit(solution)/shard_map/pallas_call | solution.py:443
  104.3 1.5 %copy.17 = bf16[64,512]{1,0:T(8,128)(2,1)} copy(bf16[64,512]{1,0:T(8,128)(2,1)} %get-tuple-element.12) | data formatting | bytes 131072
  105.8 1.1 %copy.18 = f32[64]{0:T(128)} copy(f32[64]{0:T(128)} %bitcast.10) | data formatting | bytes 512

commit v3 on v2

v3 whole, which is shorter than its diff:
```python
import itertools

import jax
import jax.numpy as jnp
from jax import lax
from jax.experimental import pallas as pl
from jax.experimental.pallas import tpu as pltpu
from jax.sharding import PartitionSpec as P

ACTIONS = 512
STATIONS = 512
EPI_BLK = 8
STEPS = 64
D = 4096
MESH = pl.DeviceIdType.MESH
NY, NX, NZ = 4, 4, 8
ROWS = 32
HALF = 256
PART = 128

step_length = 8.0


class Place:
    def __init__(self):
        grp, shard = lax.axis_index("grp"), lax.axis_index("fsdp")
        self.core = lax.rem(grp, 2)
        self.y = lax.div(grp, 2) * 2 + lax.div(shard, 32)
        self.x = lax.rem(lax.div(shard, 8), 4)
        self.z = lax.rem(shard, 8)
        self.y_hi = lax.div(grp, 2)
        self.shard = shard

    def at(self, y=None, x=None, z=None, core=None):
        y = self.y if y is None else y
        x = self.x if x is None else x
        z = self.z if z is None else z
        core = self.core if core is None else core
        return (lax.div(y, 2) * 2 + core, lax.rem(y, 2) * 32 + x * 8 + z)

    def sibling(self):
        return self.at(core=1 - self.core)

    def along_z(self, k):
        return self.at(z=lax.rem(self.z + k, NZ))

    def along_y(self, k):
        return self.at(y=lax.rem(self.y + k, NY))

    def along_x(self, k):
        return self.at(x=lax.rem(self.x + k, NX))


def greet(here):
    barrier = pltpu.get_barrier_semaphore()
    friends = [here.along_z(k) for k in range(1, NZ)]
    friends += [here.along_y(k) for k in range(1, NY)] + [here.along_x(k) for k in range(1, NX)]
    friends += [here.sibling()]
    for friend in friends:
        pl.semaphore_signal(barrier, inc=1, device_id=friend, device_id_type=MESH)
    return lambda: pl.semaphore_wait(barrier, len(friends))


def send(src, dst, sems, index, device):
    copy = pltpu.make_async_remote_copy(
        src_ref=src,
        dst_ref=dst,
        send_sem=sems[0].at[index],
        recv_sem=sems[1].at[index],
        device_id=device,
        device_id_type=MESH,
    )
    copy.start()
    return copy


def together(*walks):
    for _ in itertools.zip_longest(*walks):
        pass


GATHER_SEMS = 7 + 3 + 12 + 16


def gather_part(buf, outer, inner, along_outer, along_inner, here, sems, base):
    core, z = here.core, here.z
    numbers = itertools.count(base)
    sends, shared = [], []
    plus, minus = along_outer(1), along_outer(3)

    def put(block, device):
        copy = send(block, block, sems, next(numbers), device)
        sends.append(copy)
        return copy

    def share(block):
        shared.append(send(block, block, sems, next(numbers), here.sibling()))

    def spot(dy, dx):
        return buf.at[core, lax.rem(outer + dy, 4), lax.rem(inner + dx, 4)]

    mine = buf.at[core, outer, inner, z]
    along_z = [put(mine, here.along_z(k)) for k in (1, 7, 2, 6, 3, 5, 4)]
    yield
    for copy in along_z:
        copy.wait_recv()
    inside = {4 - k: put(spot(0, 0), along_inner(k)) for k in (1, 3, 2)}
    up, down = {0: put(spot(0, 0), plus)}, {0: put(spot(0, 0), minus)}
    share(spot(0, 0))
    onward = []

    def spread(k):
        inside[k].wait_recv()
        up[k], down[k] = put(spot(0, k), plus), put(spot(0, k), minus)
        if k == 2:
            onward.append((k, put(spot(0, k), along_outer(2))))
        share(spot(0, k))

    def from_below(k):
        up[k].wait_recv()
        if k in (0, 3):
            onward.append((k, put(spot(3, k), plus)))
        share(spot(3, k))

    def from_above(k):
        down[k].wait_recv()
        if k == 1:
            onward.append((k, put(spot(1, k), minus)))
        share(spot(1, k))

    yield
    spread(1)
    yield
    spread(3)
    yield
    from_below(0)
    yield
    spread(2)
    for k in (1, 3, 2):
        yield
        from_above(k)
        yield
        from_below(k)
    yield
    from_above(0)
    for k, copy in sorted(onward, key=lambda one: one[0] == 2):
        yield
        copy.wait_recv()
        share(spot(2, k))
    yield
    for copy in shared:
        copy.wait_recv()
    for copy in sends + shared:
        copy.wait_send()


def gather_walk(buf_a, buf_b, here, sems):
    return itertools.zip_longest(
        gather_part(buf_a, here.y, here.x, here.along_y, here.along_x, here, sems, 0),
        gather_part(buf_b, here.x, here.y, here.along_x, here.along_y, here, sems, GATHER_SEMS),
    )


SUM_SEMS = 12 + 3 + 7


def sum_part(total, outer, inner, along_outer, along_inner, bufs, here, sems, base):
    out1, in1, out2, in2, out3, in3 = bufs
    plus, minus = along_outer(1), along_outer(3)
    sends = []

    def block(dy, dx):
        return total.at[lax.rem(outer + dy, 4), lax.rem(inner + dx, 4)]

    def post(out, come, slot, value, device, number):
        out[slot] = value.astype(jnp.bfloat16)
        copy = send(out.at[slot], come.at[slot], sems, base + number, device)
        sends.append(copy)
        return copy

    def ring(slot, value, device):
        return post(out1, in1, slot, value, device, slot)

    def got(come, slot):
        return come[slot].astype(jnp.float32)

    order = (2, 1, 3, 0)
    spots = {k: i for i, k in enumerate(order)}
    up, down = (plus, minus, 1, 3), (minus, plus, 3, 1)
    way = {2: up, 0: up, 1: down, 3: down}
    first, direct, last = {}, {}, {}

    def post_first(k):
        first[k] = ring(spots[k], block(2, k)[...], way[k][0])

    def post_direct(k):
        direct[k] = ring(4 + spots[k], block(way[k][3], k)[...], way[k][1])

    inside = {}

    def finish(i, k):
        last[k].wait_recv()
        direct[k].wait_recv()
        value = block(0, k)[...] + got(in1, 4 + i) + got(in1, 8 + i)
        if k == 0:
            block(0, 0)[...] = value
        else:
            inside[k] = post(out2, in2, k - 1, value, along_inner(k), 11 + k)

    def rest():
        for i, k in enumerate(order):
            yield
            first[k].wait_recv()
            last[k] = ring(8 + i, block(way[k][2], k)[...] + got(in1, i), way[k][0])
        for i, k in enumerate(order):
            yield
            finish(i, k)
        for k in (1, 3, 2):
            yield
            inside[k].wait_recv()
            block(0, 0)[...] = block(0, 0)[...] + got(in2, k - 1)
        along_z = []
        for k in (1, 7, 2, 6, 3, 5, 4):
            value = total[outer, inner, lax.rem(here.z + k, NZ)]
            along_z.append((k, post(out3, in3, k - 1, value, here.along_z(k), 14 + k)))
        yield
        value = total[outer, inner, here.z]
        for k, copy in along_z:
            copy.wait_recv()
            value = value + got(in3, k - 1)
        total[outer, inner, here.z] = value
        for copy in sends:
            copy.wait_send()

    return post_first, post_direct, rest


def part_buffers():
    bf = jnp.bfloat16
    return [
        pltpu.VMEM((12, NZ, ROWS, PART), bf),
        pltpu.VMEM((12, NZ, ROWS, PART), bf),
        pltpu.VMEM((3, NZ, ROWS, PART), bf),
        pltpu.VMEM((3, NZ, ROWS, PART), bf),
        pltpu.VMEM((NZ - 1, ROWS, PART), bf),
        pltpu.VMEM((NZ - 1, ROWS, PART), bf),
    ]


TILE = 256
WIDE = 1024


def one_hot(column, count):
    spots = lax.broadcasted_iota(jnp.int32, (column.shape[0], count), 1).astype(jnp.float32)
    return column == spots


def columns_of(rows):
    return jnp.transpose(rows)


def advantage_of(returns, episode):
    baseline = jnp.zeros_like(returns)
    for number in range(EPI_BLK):
        member = (episode == number).astype(jnp.float32)
        total = jnp.sum(returns * member, keepdims=True)
        count = jnp.sum(member, keepdims=True)
        baseline = baseline + member * (total / count)
    return returns - baseline


def station_rows(rows_ref, tokens, table, gain, mixed, step):
    n = rows_ref.shape[0]
    lookup = one_hot(tokens, STATIONS).astype(jnp.bfloat16)
    power = jnp.zeros((n, 1), jnp.float32)
    for left in range(0, D, WIDE):
        cols = pl.ds(left, WIDE)
        value = rows_ref[:, cols].astype(jnp.float32) + jnp.dot(
            lookup, table[:, cols], preferred_element_type=jnp.float32
        )
        mixed[:n, cols] = value
        power = power + jnp.sum(value * value, axis=-1, keepdims=True)
        step()
    inverse = lax.rsqrt(power * (1.0 / D) + 1e-05)
    for left in range(0, D, WIDE):
        cols = pl.ds(left, WIDE)
        rows_ref[:, cols] = (mixed[:n, cols] * inverse * gain[:, cols]).astype(jnp.bfloat16)
    step()


def whole_kernel(
    hidden_hbm,
    roll_hbm,
    table_hbm,
    gain_hbm,
    tokens_hbm,
    action_hbm,
    roll_tokens_hbm,
    roll_action_hbm,
    returns_hbm,
    episode_hbm,
    shard_hbm,
    new_hbm,
    logp_hbm,
    episode_logp_hbm,
    gain,
    ints,
    roll_ints,
    returns,
    episode,
    shard,
    new_ref,
    logp_ref,
    episode_ref,
    features,
    rollout,
    table,
    mixed,
    scores,
    head,
    out0,
    in0,
    total_a,
    total_b,
    *rest,
):
    bufs_a, bufs_b = rest[:6], rest[6:12]
    head_a, head_b, buf_a, buf_b = rest[12:16]
    load_sem, pair_send, pair_recv, sum_send, sum_recv = rest[16:21]
    head_send, head_recv, all_send, all_recv = rest[21:]
    here = Place()
    met = greet(here)

    loads = [pltpu.make_async_copy(table_hbm, table, load_sem.at[0])]
    tiles = [pl.ds(TILE * i, TILE) for i in range(4)]
    for i, rows in enumerate(tiles):
        loads.append(
            pltpu.make_async_copy(hidden_hbm.at[rows], features.at[rows], load_sem.at[1 + i])
        )
    loads.append(pltpu.make_async_copy(roll_hbm, rollout, load_sem.at[5]))
    small = [
        (shard_hbm, shard),
        (tokens_hbm, ints.at[0:8]),
        (action_hbm, ints.at[8:16]),
        (roll_tokens_hbm, roll_ints.at[0]),
        (roll_action_hbm, roll_ints.at[1]),
        (returns_hbm, returns),
        (episode_hbm, episode),
        (gain_hbm, gain),
    ]
    small = [
        pltpu.make_async_copy(src, dst, load_sem.at[6 + i]) for i, (src, dst) in enumerate(small)
    ]
    for load in small:
        load.start()
    loads[0].start()
    loads[1].start()

    small[0].wait()
    rows = pl.ds(pl.multiple_of(here.y_hi * ROWS, ROWS), ROWS)
    for part, (buf, spot) in enumerate(((head_a, (here.y, here.x)), (head_b, (here.x, here.y)))):
        cols = pl.ds(pl.multiple_of(here.core * HALF + part * PART, PART), PART)
        buf[here.core, spot[0], spot[1], here.z] = shard[rows, cols]
    met()
    walk = gather_walk(head_a, head_b, here, (head_send, head_recv))
    next(walk)
    turn = itertools.count(1)

    def step():
        if next(turn) in (6, 9, 10, 11, 12, 13, 14, 15, 16, 17, 18, 19, 20, 21, 22, 23):
            next(walk, None)

    for load in small[1:]:
        load.wait()
    numbers = columns_of(ints[...].astype(jnp.float32))
    beside = jnp.concatenate([roll_ints[0], roll_ints[1]], axis=1).astype(jnp.float32)
    roll_numbers = columns_of(jnp.broadcast_to(beside, (8, 128)))
    advantage = columns_of(advantage_of(returns[...], episode[...]))

    def column(values, first, tile):
        return jnp.concatenate([values[:, first + 2 * tile + j][:, None] for j in range(2)], axis=0)

    loads[0].wait()
    for i, rows in enumerate(tiles):
        loads[2 + i].start()
        loads[1 + i].wait()
        station_rows(features.at[rows], column(numbers, 0, i), table, gain, mixed, step)
    loads[5].wait()
    station_rows(rollout, roll_numbers[:STEPS, :1], table, gain, mixed, step)
    for _ in walk:
        pass
    for core, y, x in itertools.product(range(2), range(NY), range(NX)):
        for part, blocks in enumerate((head_a[core, y, x], head_b[core, x, y])):
            head[y % 2, x, :, y // 2, :, pl.ds(core * HALF + part * PART, PART)] = blocks

    for i, rows in enumerate(tiles):
        logits = jnp.dot(
            features[rows, :],
            head[...].reshape(D, ACTIONS),
            preferred_element_type=jnp.float32,
        )
        expo = jnp.exp(logits - jnp.max(logits, axis=-1, keepdims=True))
        probs = expo / jnp.sum(expo, axis=-1, keepdims=True)
        chosen = one_hot(column(numbers, 8, i), ACTIONS).astype(jnp.float32)
        value = (column(advantage, 0, i) * (probs - chosen)).astype(jnp.bfloat16)
        scores[0, rows] = value[:, :HALF]
        scores[1, rows] = value[:, HALF:]

    sems = (sum_send, sum_recv)
    first_a, direct_a, rest_a = sum_part(
        total_a, here.y, here.x, here.along_y, here.along_x, bufs_a, here, sems, 0
    )
    first_b, direct_b, rest_b = sum_part(
        total_b, here.x, here.y, here.along_x, here.along_y, bufs_b, here, sems, SUM_SEMS
    )
    pairs = []
    mine, theirs = scores[here.core], scores[1 - here.core]

    def chunk(far, dx):
        y_lo = lax.rem(here.y + far, 2)
        return y_lo, lax.rem(here.x + dx, NX)

    def make(far, dx):
        y_lo, x = chunk(far, dx)
        cols = pl.ds(pl.multiple_of(y_lo * (D // 2) + x * 512, 512), 512)
        left = jnp.transpose(features[:, cols])
        k = len(pairs)
        out0[k] = jnp.dot(left, theirs, preferred_element_type=jnp.float32).astype(jnp.bfloat16)
        pairs.append(send(out0.at[k], in0.at[k], (pair_send, pair_recv), k, here.sibling()))
        own = jnp.dot(left, mine, preferred_element_type=jnp.float32).reshape(NZ, 2, ROWS, HALF)
        for y_hi in range(2):
            total_a[2 * y_hi + y_lo, x] = own[:, y_hi, :, :PART]
            total_b[x, 2 * y_hi + y_lo] = own[:, y_hi, :, PART:]

    def both(k, far, dx):
        y_lo, x = chunk(far, dx)
        pairs[k].wait_recv()
        other = in0[k].astype(jnp.float32).reshape(NZ, 2, ROWS, HALF)
        for y_hi in range(2):
            y = 2 * y_hi + y_lo
            total_a[y, x] = total_a[y, x] + other[:, y_hi, :, :PART]
            total_b[x, y] = total_b[x, y] + other[:, y_hi, :, PART:]

    ready = [
        ((0, 2), [(first_b, 2), (first_a, 2), (first_b, 0)]),
        ((1, 2), [(first_b, 1), (first_b, 3), (direct_a, 2)]),
        ((0, 1), [(first_a, 1)]),
        ((0, 3), [(first_a, 3), (direct_b, 2), (direct_b, 0)]),
        ((0, 0), [(first_a, 0)]),
        ((1, 1), [(direct_a, 1), (direct_b, 1), (direct_b, 3)]),
        ((1, 3), [(direct_a, 3)]),
        ((1, 0), [(direct_a, 0)]),
    ]

    def settle(k):
        both(k, *ready[k][0])
        for post, distance in ready[k][1]:
            post(distance)

    summing = itertools.zip_longest(rest_a(), rest_b())
    next(summing)
    for k, (where, _) in enumerate(ready):
        make(*where)
        if k:
            settle(k - 1)
        if k >= 6:
            next(summing)
    settle(7)
    for copy in pairs:
        copy.wait_send()

    for _ in summing:
        pass

    buf_a[here.core, here.y, here.x, here.z] = total_a[here.y, here.x, here.z].astype(jnp.bfloat16)
    buf_b[here.core, here.x, here.y, here.z] = total_b[here.x, here.y, here.z].astype(jnp.bfloat16)
    for _ in gather_walk(buf_a, buf_b, here, (all_send, all_recv)):
        pass

    squares = jnp.zeros((ROWS, PART), jnp.float32)
    for core, y, x in itertools.product(range(2), range(NY), range(NX)):
        for block in (buf_a[core, y, x], buf_b[core, x, y]):
            block = block.astype(jnp.float32)
            squares = squares + jnp.sum(block * block, axis=0)
    scale = step_length * lax.rsqrt(jnp.sum(squares, keepdims=True) + 1e-06)
    for core, y, x in itertools.product(range(2), range(NY), range(NX)):
        for part, block in enumerate((buf_a[core, y, x], buf_b[core, x, y])):
            cols = pl.ds(core * HALF + part * PART, PART)
            old = head[y % 2, x, :, y // 2, :, cols].astype(jnp.float32)
            change = block.astype(jnp.float32) * scale.reshape(1, 1, 1)
            head[y % 2, x, :, y // 2, :, cols] = (old - change).astype(jnp.bfloat16)
    new_ref[...] = head[lax.rem(here.y, 2), here.x, here.z].reshape(2 * ROWS, ACTIONS)
    new_store = pltpu.make_async_copy(new_ref, new_hbm, load_sem.at[2])
    new_store.start()
    logits = jnp.dot(
        rollout[...], head[...].reshape(D, ACTIONS), preferred_element_type=jnp.float32
    )
    top = jnp.max(logits, axis=-1, keepdims=True)
    total = jnp.log(jnp.sum(jnp.exp(logits - top), axis=-1, keepdims=True)) + top
    chosen = one_hot(roll_numbers[STEPS:, :1], ACTIONS).astype(jnp.float32)
    logp = jnp.sum(logits * chosen, axis=-1, keepdims=True) - total
    logp_ref[...] = jnp.transpose(jnp.broadcast_to(logp, (STEPS, 128)))[:1, :]
    episode_ref[...] = jnp.broadcast_to(jnp.sum(logp, keepdims=True), (1, 128))
    stores = [
        pltpu.make_async_copy(src, dst, load_sem.at[i])
        for i, (src, dst) in enumerate(((logp_ref, logp_hbm), (episode_ref, episode_logp_hbm)))
    ]
    for store in stores:
        store.start()
    for store in stores + [new_store]:
        store.wait()


SPREAD = (2, NX, NZ, 2, ROWS, ACTIONS)


def dma_sems(count):
    return [pltpu.SemaphoreType.DMA((count,)), pltpu.SemaphoreType.DMA((count,))]


def gather_buffers():
    return [
        pltpu.VMEM((2, NY, NX, NZ, ROWS, PART), jnp.bfloat16),
        pltpu.VMEM((2, NX, NY, NZ, ROWS, PART), jnp.bfloat16),
    ]


def hand_over(*refs):
    for source, target in zip(refs[:3], refs[3:]):
        target[...] = source[...]


def results(*arrays):
    vmem = pl.BlockSpec(memory_space=pltpu.VMEM)
    return pl.pallas_call(
        hand_over,
        out_shape=tuple(jax.ShapeDtypeStruct(a.shape, a.dtype) for a in arrays),
        in_specs=[vmem] * 3,
        out_specs=(vmem,) * 3,
    )(*arrays)


def whole_step(*arrays):
    anywhere = pl.BlockSpec(memory_space=pl.ANY)
    return pl.pallas_call(
        whole_kernel,
        out_shape=(
            jax.ShapeDtypeStruct((2 * ROWS, ACTIONS), jnp.bfloat16),
            jax.ShapeDtypeStruct((1, STEPS), jnp.float32),
            jax.ShapeDtypeStruct((1, 128), jnp.float32),
        ),
        in_specs=[anywhere] * len(arrays),
        out_specs=(anywhere,) * 3,
        scratch_shapes=[
            pltpu.VMEM((1, D), jnp.float32),
            pltpu.VMEM((16, 128), jnp.int32),
            pltpu.VMEM((2, 1, STEPS), jnp.int32),
            pltpu.VMEM((8, 128), jnp.float32),
            pltpu.VMEM((8, 128), jnp.int32),
            pltpu.VMEM((2 * ROWS, ACTIONS), jnp.bfloat16),
            pltpu.VMEM((2 * ROWS, ACTIONS), jnp.bfloat16),
            pltpu.VMEM((1, STEPS), jnp.float32),
            pltpu.VMEM((1, 128), jnp.float32),
            pltpu.VMEM((1024, D), jnp.bfloat16),
            pltpu.VMEM((STEPS, D), jnp.bfloat16),
            pltpu.VMEM((STATIONS, D), jnp.bfloat16),
            pltpu.VMEM((TILE, D), jnp.float32),
            pltpu.VMEM((2, 1024, HALF), jnp.bfloat16),
            pltpu.VMEM(SPREAD, jnp.bfloat16),
            pltpu.VMEM((8, 512, HALF), jnp.bfloat16),
            pltpu.VMEM((8, 512, HALF), jnp.bfloat16),
            pltpu.VMEM((NY, NX, NZ, ROWS, PART), jnp.float32),
            pltpu.VMEM((NX, NY, NZ, ROWS, PART), jnp.float32),
            *part_buffers(),
            *part_buffers(),
            *gather_buffers(),
            *gather_buffers(),
            pltpu.SemaphoreType.DMA((14,)),
            *dma_sems(8),
            *dma_sems(2 * SUM_SEMS),
            *dma_sems(2 * GATHER_SEMS),
            *dma_sems(2 * GATHER_SEMS),
        ],
        compiler_params=pltpu.CompilerParams(
            collective_id=0, has_side_effects=True, vmem_limit_bytes=60 << 20
        ),
    )(*arrays)


def local(
    traj_hidden,
    traj_tokens,
    traj_action,
    traj_return,
    traj_episode,
    roll_hidden,
    roll_tokens,
    roll_action,
    station_table,
    norm_gain,
    head_weight,
):
    arrays = whole_step(
        traj_hidden,
        roll_hidden,
        station_table,
        norm_gain.reshape(1, D),
        traj_tokens.reshape(8, 128),
        traj_action.reshape(8, 128),
        roll_tokens.reshape(1, STEPS),
        roll_action.reshape(1, STEPS),
        traj_return.reshape(8, 128),
        traj_episode.reshape(8, 128),
        head_weight,
    )
    new_head, action_logp, episode_logp = results(*arrays)
    return (new_head, action_logp.reshape(STEPS), episode_logp[0, :1])


def solution(mesh):
    placed = (
        P(("grp", "fsdp"), None),
        P(("grp", "fsdp")),
        P(("grp", "fsdp")),
        P(("grp", "fsdp")),
        P(("grp", "fsdp"), None),
        P(("grp", "fsdp"), None),
        P(("grp", "fsdp")),
        P(("grp", "fsdp")),
        P(),
        P(),
        P("fsdp", None),
    )
    return jax.shard_map(
        local,
        mesh=mesh,
        in_specs=placed,
        out_specs=(P("fsdp", None), P(("grp", "fsdp")), P(("grp", "fsdp"))),
        check_vma=False,
    )
```

time: 109 us -> 92.6 us (0.85)
  Pallas kernels: 102 us -> 91.9 us
  local copies, waits for them, and re-layouts: 3.98 us -> 0 us
  between operations: 2.33 us -> 0.64 us
    pallas_call x1 -> x2, Pallas kernels: 102 us -> 91.9 us  [the longest x1 90.4 us: whole_step(): pl.pallas_call(whole_kernel, out_shape=(jax.ShapeDtypeStruct((2 * ROWS, A...]
    unnamed x2 -> x0, local copies, waits for them, and re-layouts: 2.59 us -> none
where the time goes in v3:
time: 92.6 us; the launch traced here: 92.5 us
  Pallas kernels  91.9 us (99%)
    pallas_call x1, Pallas kernels, whole_step(): pl.pallas_call(whole_kernel, out_shape=(jax.ShapeDtypeStruct((2 * ROWS, A...  90.4 us

profile of v3, /device:TPU:1, one launch (start us, length us, event | category | flops | bytes accessed | tf_op | source)
XLA Modules:
  0.0 92.5 jit_solution(10783759320141408833)
XLA Ops:
  0.6 90.4 %shard_map.130 = (bf16[64,512]{1,0:T(8,128)(2,1)}, f32[1,64]{1,0:T(1,128)}, f32[1,128]{1,0:T(1,128)}) custom-call(bf16[1024,4096]{1,0:T(8,128)(2,1)} %hidden_hbm.1, bf16[64,4096]{1,0:T(8,128)(2,1)} %roll_hbm.1, bf16[512,4096]{1,0:T(8,128)(2,1)} %table_hbm.1, f32[1,4096]{1,0:T(1,128)} %bitcast.10, s32[8,128]{1,0:T(8,128)} %bitcast.11, s32[8,128]{1,0:T(8,128)} %bitcast.12, ...), custom_call_target="tpu_custom_call" | custom-call | tf_op jit(solution)/shard_map/pallas_call | solution.py:546
  91.0 1.5 %shard_map.131 = (bf16[64,512]{1,0:T(8,128)(2,1)}, f32[1,64]{1,0:T(1,128)}, f32[1,128]{1,0:T(1,128)}) custom-call(bf16[64,512]{1,0:T(8,128)(2,1)} %get-tuple-element.9.refs_0_, f32[1,64]{1,0:T(1,128)} %get-tuple-element.10.refs_1_, f32[1,128]{1,0:T(1,128)} %get-tuple-element.11.refs_2_), custom_call_target="tpu_custom_call" | custom-call | tf_op jit(solution)/shard_map/pallas_call | solution.py:536

commit v4 on v3

--- a/solution.py
+++ b/solution.py
@@ -82,10 +82,10 @@
 GATHER_SEMS = 7 + 3 + 12 + 16
 
 
-def gather_part(buf, outer, inner, along_outer, along_inner, here, sems, base):
+def gather_part(buf, outer, inner, along_outer, along_inner, here, sems, base, landed=None):
     core, z = here.core, here.z
     numbers = itertools.count(base)
-    sends, shared = [], []
+    sends, shared, waiting = [], [], []
     plus, minus = along_outer(1), along_outer(3)
 
     def put(block, device):
@@ -93,8 +93,23 @@
         sends.append(copy)
         return copy
 
-    def share(block):
-        shared.append(send(block, block, sems, next(numbers), here.sibling()))
+    def report(which, dy, dx):
+        if landed is not None:
+            landed(which, lax.rem(outer + dy, 4), lax.rem(inner + dx, 4))
+
+    def receive():
+        dy, dx, copy = waiting.pop(0)
+        copy.wait_recv()
+        report(1 - core, dy, dx)
+
+    def share(dy, dx):
+        block = spot(dy, dx)
+        copy = send(block, block, sems, next(numbers), here.sibling())
+        shared.append(copy)
+        waiting.append((dy, dx, copy))
+        report(core, dy, dx)
+        if landed is not None and len(waiting) > 4:
+            receive()
 
     def spot(dy, dx):
         return buf.at[core, lax.rem(outer + dy, 4), lax.rem(inner + dx, 4)]
@@ -106,7 +121,7 @@
         copy.wait_recv()
     inside = {4 - k: put(spot(0, 0), along_inner(k)) for k in (1, 3, 2)}
     up, down = {0: put(spot(0, 0), plus)}, {0: put(spot(0, 0), minus)}
-    share(spot(0, 0))
+    share(0, 0)
     onward = []
 
     def spread(k):
@@ -114,19 +129,19 @@
         up[k], down[k] = put(spot(0, k), plus), put(spot(0, k), minus)
         if k == 2:
             onward.append((k, put(spot(0, k), along_outer(2))))
-        share(spot(0, k))
+        share(0, k)
 
     def from_below(k):
         up[k].wait_recv()
         if k in (0, 3):
             onward.append((k, put(spot(3, k), plus)))
-        share(spot(3, k))
+        share(3, k)
 
     def from_above(k):
         down[k].wait_recv()
         if k == 1:
             onward.append((k, put(spot(1, k), minus)))
-        share(spot(1, k))
+        share(1, k)
 
     yield
     spread(1)
@@ -146,18 +161,19 @@
     for k, copy in sorted(onward, key=lambda one: one[0] == 2):
         yield
         copy.wait_recv()
-        share(spot(2, k))
+        share(2, k)
     yield
-    for copy in shared:
-        copy.wait_recv()
+    while waiting:
+        receive()
     for copy in sends + shared:
         copy.wait_send()
 
 
-def gather_walk(buf_a, buf_b, here, sems):
+def gather_walk(buf_a, buf_b, here, sems, landed_a=None, landed_b=None):
+    y, x = (here.y, here.along_y), (here.x, here.along_x)
     return itertools.zip_longest(
-        gather_part(buf_a, here.y, here.x, here.along_y, here.along_x, here, sems, 0),
-        gather_part(buf_b, here.x, here.y, here.along_x, here.along_y, here, sems, GATHER_SEMS),
+        gather_part(buf_a, y[0], x[0], y[1], x[1], here, sems, 0, landed_a),
+        gather_part(buf_b, x[0], y[0], x[1], y[1], here, sems, GATHER_SEMS, landed_b),
     )
 
 
@@ -319,6 +335,7 @@
     mixed,
     scores,
     head,
+    squares,
     out0,
     in0,
     total_a,
@@ -470,30 +487,45 @@
     for copy in pairs:
         copy.wait_send()
 
-    for _ in summing:
-        pass
+    for turn, _ in enumerate(summing):
+        if turn == 8:
+            mixed[:STEPS, :ACTIONS] = jnp.dot(
+                rollout[...], head[...].reshape(D, ACTIONS), preferred_element_type=jnp.float32
+            )
+            shard[...] = head[lax.rem(here.y, 2), here.x, here.z].reshape(2 * ROWS, ACTIONS)
 
     buf_a[here.core, here.y, here.x, here.z] = total_a[here.y, here.x, here.z].astype(jnp.bfloat16)
     buf_b[here.core, here.x, here.y, here.z] = total_b[here.x, here.y, here.z].astype(jnp.bfloat16)
-    for _ in gather_walk(buf_a, buf_b, here, (all_send, all_recv)):
+
+    def landing(part, buf, y_first):
+        def landed(core, a, b):
+            y, x = (a, b) if y_first else (b, a)
+            block = buf[core, a, b]
+            cols = pl.ds(pl.multiple_of(core * HALF + part * PART, PART), PART)
+            head[lax.rem(y, 2), x, :, lax.div(y, 2), :, cols] = block
+            block = block.astype(jnp.float32)
+            squares[core, part, y, x] = jnp.sum((block * block).reshape(-1, 8, PART), axis=0)
+
+        return landed
+
+    for _ in gather_walk(
+        buf_a,
+        buf_b,
+        here,
+        (all_send, all_recv),
+        landing(0, buf_a, True),
+        landing(1, buf_b, False),
+    ):
         pass
 
-    squares = jnp.zeros((ROWS, PART), jnp.float32)
-    for core, y, x in itertools.product(range(2), range(NY), range(NX)):
-        for block in (buf_a[core, y, x], buf_b[core, x, y]):
-            block = block.astype(jnp.float32)
-            squares = squares + jnp.sum(block * block, axis=0)
-    scale = step_length * lax.rsqrt(jnp.sum(squares, keepdims=True) + 1e-06)
-    for core, y, x in itertools.product(range(2), range(NY), range(NX)):
-        for part, block in enumerate((buf_a[core, y, x], buf_b[core, x, y])):
-            cols = pl.ds(core * HALF + part * PART, PART)
-            old = head[y % 2, x, :, y // 2, :, cols].astype(jnp.float32)
-            change = block.astype(jnp.float32) * scale.reshape(1, 1, 1)
-            head[y % 2, x, :, y // 2, :, cols] = (old - change).astype(jnp.bfloat16)
-    new_ref[...] = head[lax.rem(here.y, 2), here.x, here.z].reshape(2 * ROWS, ACTIONS)
+    scale = step_length * lax.rsqrt(jnp.sum(squares[...], keepdims=True).reshape(1, 1) + 1e-06)
+    change = head[lax.rem(here.y, 2), here.x, here.z].reshape(2 * ROWS, ACTIONS)
+    new_ref[...] = (
+        shard[...].astype(jnp.float32) - change.astype(jnp.float32) * scale
+    ).astype(jnp.bfloat16)
     new_store = pltpu.make_async_copy(new_ref, new_hbm, load_sem.at[2])
     new_store.start()
-    logits = jnp.dot(
+    logits = mixed[:STEPS, :ACTIONS] - scale * jnp.dot(
         rollout[...], head[...].reshape(D, ACTIONS), preferred_element_type=jnp.float32
     )
     top = jnp.max(logits, axis=-1, keepdims=True)
@@ -568,6 +600,7 @@
             pltpu.VMEM((TILE, D), jnp.float32),
             pltpu.VMEM((2, 1024, HALF), jnp.bfloat16),
             pltpu.VMEM(SPREAD, jnp.bfloat16),
+            pltpu.VMEM((2, 2, NY, NX, 8, PART), jnp.float32),
             pltpu.VMEM((8, 512, HALF), jnp.bfloat16),
             pltpu.VMEM((8, 512, HALF), jnp.bfloat16),
             pltpu.VMEM((NY, NX, NZ, ROWS, PART), jnp.float32),

time: 92.6 us -> 90.3 us (0.975)
  Pallas kernels: 91.9 us -> 89.5 us
    pallas_call x1, Pallas kernels: 90.4 us -> 88.1 us  [whole_step(): pl.pallas_call(whole_kernel, out_shape=(jax.ShapeDtypeStruct((2 * ROWS, A...]
where the time goes in v4:
time: 90.3 us; the launch traced here: 90.2 us
  Pallas kernels  89.5 us (99%)
    pallas_call x1, Pallas kernels, whole_step(): pl.pallas_call(whole_kernel, out_shape=(jax.ShapeDtypeStruct((2 * ROWS, A...  88.1 us

profile of v4, /device:TPU:1, one launch (start us, length us, event | category | flops | bytes accessed | tf_op | source)
XLA Modules:
  0.0 90.2 jit_solution(16458528494890529020)
XLA Ops:
  0.6 88.1 %shard_map.130 = (bf16[64,512]{1,0:T(8,128)(2,1)}, f32[1,64]{1,0:T(1,128)}, f32[1,128]{1,0:T(1,128)}) custom-call(bf16[1024,4096]{1,0:T(8,128)(2,1)} %hidden_hbm.1, bf16[64,4096]{1,0:T(8,128)(2,1)} %roll_hbm.1, bf16[512,4096]{1,0:T(8,128)(2,1)} %table_hbm.1, f32[1,4096]{1,0:T(1,128)} %bitcast.10, s32[8,128]{1,0:T(8,128)} %bitcast.11, s32[8,128]{1,0:T(8,128)} %bitcast.12, ...), custom_call_target="tpu_custom_call" | custom-call | tf_op jit(solution)/shard_map/pallas_call | solution.py:578
  88.7 1.5 %shard_map.131 = (bf16[64,512]{1,0:T(8,128)(2,1)}, f32[1,64]{1,0:T(1,128)}, f32[1,128]{1,0:T(1,128)}) custom-call(bf16[64,512]{1,0:T(8,128)(2,1)} %get-tuple-element.9.refs_0_, f32[1,64]{1,0:T(1,128)} %get-tuple-element.10.refs_1_, f32[1,128]{1,0:T(1,128)} %get-tuple-element.11.refs_2_), custom_call_target="tpu_custom_call" | custom-call | tf_op jit(solution)/shard_map/pallas_call | solution.py:568

commit v5 on v4

--- a/solution.py
+++ b/solution.py
@@ -151,13 +151,17 @@
     from_below(0)
     yield
     spread(2)
-    for k in (1, 3, 2):
+    for take, k in (
+        (from_above, 1),
+        (from_below, 3),
+        (from_above, 0),
+        (from_below, 1),
+        (from_above, 3),
+        (from_below, 2),
+        (from_above, 2),
+    ):
         yield
-        from_above(k)
-        yield
-        from_below(k)
-    yield
-    from_above(0)
+        take(k)
     for k, copy in sorted(onward, key=lambda one: one[0] == 2):
         yield
         copy.wait_recv()

time: 90.3 us -> 90.1 us (level)
  no operation moved by 1% of the time
where the time goes in v5:
time: 90.1 us; the launch traced here: 90 us
  Pallas kernels  89.4 us (99%)
    pallas_call x1, Pallas kernels, whole_step(): pl.pallas_call(whole_kernel, out_shape=(jax.ShapeDtypeStruct((2 * ROWS, A...  87.9 us

profile of v5, /device:TPU:1, one launch (start us, length us, event | category | flops | bytes accessed | tf_op | source)
XLA Modules:
  0.0 90.0 jit_solution(11149755176133574851)
XLA Ops:
  0.6 87.9 %shard_map.130 = (bf16[64,512]{1,0:T(8,128)(2,1)}, f32[1,64]{1,0:T(1,128)}, f32[1,128]{1,0:T(1,128)}) custom-call(bf16[1024,4096]{1,0:T(8,128)(2,1)} %hidden_hbm.1, bf16[64,4096]{1,0:T(8,128)(2,1)} %roll_hbm.1, bf16[512,4096]{1,0:T(8,128)(2,1)} %table_hbm.1, f32[1,4096]{1,0:T(1,128)} %bitcast.10, s32[8,128]{1,0:T(8,128)} %bitcast.11, s32[8,128]{1,0:T(8,128)} %bitcast.12, ...), custom_call_target="tpu_custom_call" | custom-call | tf_op jit(solution)/shard_map/pallas_call | solution.py:582
  88.5 1.5 %shard_map.131 = (bf16[64,512]{1,0:T(8,128)(2,1)}, f32[1,64]{1,0:T(1,128)}, f32[1,128]{1,0:T(1,128)}) custom-call(bf16[64,512]{1,0:T(8,128)(2,1)} %get-tuple-element.9.refs_0_, f32[1,64]{1,0:T(1,128)} %get-tuple-element.10.refs_1_, f32[1,128]{1,0:T(1,128)} %get-tuple-element.11.refs_2_), custom_call_target="tpu_custom_call" | custom-call | tf_op jit(solution)/shard_map/pallas_call | solution.py:572
